TPU v7x, 32 devices: a whole 2x2x4 slice. The times are simulated.
32 devices in a mesh: fsdp: 8 (over z, y), tensor: 4 (over x, core).
Axes of the slice: x: 2, y: 2, z: 4, core: 2. Of those that a mesh axis runs over, the one named last changes fastest.
Arguments:
- images: bfloat16 [2, 8, 577, 1024], P(None, 'fsdp'), may hold values from -6 to 6
- cotangent: bfloat16 [2, 8, 577, 1024], P(None, 'fsdp'), may hold values from -6 to 6
- ln1_gain: bfloat16 [1024], P(('fsdp', 'tensor')), may hold values from 0.5 to 1.5
- ln1_bias: bfloat16 [1024], P(('fsdp', 'tensor')), may hold values from -3 to 3
- qkv_weight: bfloat16 [1024, 16, 192], P('fsdp', 'tensor'), may hold values from -0.1875 to 0.1875
- qv_bias: bfloat16 [16, 128], P('tensor', 'fsdp'), may hold values from -1.1953125 to 1.1953125
- out_weight: bfloat16 [1024, 1024], P('tensor', 'fsdp'), may hold values from -0.75 to 0.75
- out_bias: bfloat16 [1024], P(('fsdp', 'tensor')), may hold values from -3 to 3
- ln2_gain: bfloat16 [1024], P(('fsdp', 'tensor')), may hold values from 0.5 to 1.5
- ln2_bias: bfloat16 [1024], P(('fsdp', 'tensor')), may hold values from -3 to 3
- up_weight: bfloat16 [1024, 4096], P('fsdp', 'tensor'), may hold values from -0.1875 to 0.1875
- up_bias: bfloat16 [4, 1024], P('tensor', 'fsdp'), may hold values from -3 to 3
- down_weight: bfloat16 [4096, 1024], P('tensor', 'fsdp'), may hold values from -0.09375 to 0.09375
- down_bias: bfloat16 [1024], P(('fsdp', 'tensor')), may hold values from -3 to 3
Outputs:
- activations: bfloat16 [2, 8, 577, 1024], P(None, 'fsdp')
- input_grad: float32 [2, 8, 577, 1024], P(None, 'fsdp')
- ln1_gain_grad: float32 [1024], P(('fsdp', 'tensor'))
- ln1_bias_grad: float32 [1024], P(('fsdp', 'tensor'))
- qkv_weight_grad: float32 [1024, 16, 192], P('fsdp', 'tensor')
- qv_bias_grad: float32 [16, 128], P('tensor', 'fsdp')
- out_weight_grad: float32 [1024, 1024], P('tensor', 'fsdp')
- out_bias_grad: float32 [1024], P(('fsdp', 'tensor'))
- ln2_gain_grad: float32 [1024], P(('fsdp', 'tensor'))
- ln2_bias_grad: float32 [1024], P(('fsdp', 'tensor'))
- up_weight_grad: float32 [1024, 4096], P('fsdp', 'tensor')
- up_bias_grad: float32 [4, 1024], P('tensor', 'fsdp')
- down_weight_grad: float32 [4096, 1024], P('tensor', 'fsdp')
- down_bias_grad: float32 [1024], P(('fsdp', 'tensor'))
All inputs are finite; a program needn't handle non-finite values.
Results may differ from a plain program's by a relative error of at most 0.023.
Values may be sent and summed in bfloat16 or wider, within the bound.
No kernel may reach another device: no remote copies, remote signals or barrier semaphores. Data moves between devices by JAX's collectives and lax.ppermute only.
A program may use at most 128 MiB of HBM per device.

v0:
```python
import jax
import jax.numpy as jnp
from jax import lax
from jax.sharding import PartitionSpec as P

epsilon = 1e-06


def layer_norm(values, scale_vec, shift_vec):
    centred = values - jnp.mean(values, axis=-1, keepdims=True)
    spread = jnp.mean(centred * centred, axis=-1, keepdims=True)
    return centred * lax.rsqrt(spread + epsilon) * scale_vec + shift_vec


def gelu_exact(values):
    return jax.nn.gelu(values, approximate=False)


def unpack_attn(gathered, model_width):
    qkv_full, qv_full, out_full = gathered
    return (qkv_full.reshape(model_width, -1), qv_full.astype(jnp.float32), out_full)


def unpack_mlp(gathered):
    up_full, up_shift_full, down_full = gathered
    return (up_full, up_shift_full.reshape(-1).astype(jnp.float32), down_full)


def shards(
    images,
    cotangent,
    ln1_gain,
    ln1_bias,
    qkv_weight,
    qv_bias,
    out_weight,
    out_bias,
    ln2_gain,
    ln2_bias,
    up_weight,
    up_bias,
    down_weight,
    down_bias,
):
    micro_count, images_local, seq_len, model_width = images.shape
    row_count = images_local * seq_len
    heads_local = qkv_weight.shape[1]
    head_dim = qkv_weight.shape[2] // 3
    qkv_cols = heads_local * 3 * head_dim
    hidden_local = up_weight.shape[1]
    score_scale = head_dim ** (-0.5)
    fsdp_count = lax.axis_size("fsdp")
    tensor_count = lax.axis_size("tensor")
    f32 = jnp.float32
    bf16 = jnp.bfloat16
    vector_list = (
        lax.all_gather(ln1_gain, ("fsdp", "tensor"), axis=0, tiled=True),
        lax.all_gather(ln1_bias, ("fsdp", "tensor"), axis=0, tiled=True),
        lax.all_gather(out_bias, ("fsdp", "tensor"), axis=0, tiled=True),
        lax.all_gather(ln2_gain, ("fsdp", "tensor"), axis=0, tiled=True),
        lax.all_gather(ln2_bias, ("fsdp", "tensor"), axis=0, tiled=True),
        lax.all_gather(down_bias, ("fsdp", "tensor"), axis=0, tiled=True),
    )
    gain_one, shift_one, out_shift, gain_two, shift_two, down_shift = [
        member.astype(f32) for member in vector_list
    ]
    qkv_acc = jnp.zeros((model_width, qkv_cols), f32)
    qv_acc = jnp.zeros((heads_local, 2 * head_dim), f32)
    out_acc = jnp.zeros((heads_local * head_dim, model_width), f32)
    up_acc = jnp.zeros((model_width, hidden_local), f32)
    up_shift_acc = jnp.zeros((hidden_local,), f32)
    down_acc = jnp.zeros((hidden_local, model_width), f32)
    gain_one_acc = jnp.zeros((model_width,), f32)
    shift_one_acc = jnp.zeros((model_width,), f32)
    out_shift_acc = jnp.zeros((model_width,), f32)
    gain_two_acc = jnp.zeros((model_width,), f32)
    shift_two_acc = jnp.zeros((model_width,), f32)
    down_shift_acc = jnp.zeros((model_width,), f32)
    outputs_all = []
    grads_in_all = []
    for mb_index in range(micro_count):
        attn_full = (
            lax.all_gather(qkv_weight, "fsdp", axis=0, tiled=True),
            lax.all_gather(qv_bias, "fsdp", axis=1, tiled=True),
            lax.all_gather(out_weight, "fsdp", axis=1, tiled=True),
        )
        qkv_mat, qv_shift, out_mat = unpack_attn(attn_full, model_width)
        input_rows = images[mb_index].reshape(row_count, model_width).astype(f32)
        normed_one, norm_one_pull = jax.vjp(layer_norm, input_rows, gain_one, shift_one)
        act_one = normed_one.astype(bf16)
        projected = jnp.dot(act_one, qkv_mat, preferred_element_type=f32).reshape(
            images_local, seq_len, heads_local, 3 * head_dim
        )
        queries = (projected[..., :head_dim] + qv_shift[:, :head_dim]).astype(bf16)
        key_rows = projected[..., head_dim : 2 * head_dim].astype(bf16)
        val_rows = (projected[..., 2 * head_dim :] + qv_shift[:, head_dim:]).astype(bf16)
        scores = (
            jnp.einsum("bshd,bthd->bhst", queries, key_rows, preferred_element_type=f32)
            * score_scale
        )
        top_score = jnp.max(scores, axis=-1, keepdims=True)
        exp_scores = jnp.exp(scores - top_score)
        exp_total = jnp.sum(exp_scores, axis=-1, keepdims=True)
        logsum_exp = top_score + jnp.log(exp_total)
        weights_low = (exp_scores / exp_total).astype(bf16)
        attended = (
            jnp.einsum("bhst,bthd->bshd", weights_low, val_rows, preferred_element_type=f32)
            .astype(bf16)
            .reshape(row_count, heads_local * head_dim)
        )
        branch_part = jnp.dot(attended, out_mat, preferred_element_type=f32)
        hidden_res = input_rows + (
            lax.psum(branch_part.astype(jnp.bfloat16), "tensor").astype(jnp.float32) + out_shift
        )
        mlp_full = (
            lax.all_gather(up_weight, "fsdp", axis=0, tiled=True),
            lax.all_gather(up_bias, "fsdp", axis=1, tiled=True),
            lax.all_gather(down_weight, "fsdp", axis=1, tiled=True),
        )
        up_mat, up_shift, down_mat = unpack_mlp(mlp_full)
        normed_two, norm_two_pull = jax.vjp(layer_norm, hidden_res, gain_two, shift_two)
        act_two = normed_two.astype(bf16)
        pre_act = jnp.dot(act_two, up_mat, preferred_element_type=f32) + up_shift
        gelu_full, gelu_pull = jax.vjp(gelu_exact, pre_act)
        activated = gelu_full.astype(bf16)
        mlp_part = jnp.dot(activated, down_mat, preferred_element_type=f32)
        mlp_total = lax.psum(mlp_part.astype(jnp.bfloat16), "tensor").astype(jnp.float32)
        output_rows = (hidden_res + (mlp_total + down_shift)).astype(bf16)
        outputs_all.append(output_rows.reshape(images_local, seq_len, model_width))
        up_mat, up_shift, down_mat = unpack_mlp(
            (
                lax.all_gather(up_weight, "fsdp", axis=0, tiled=True),
                lax.all_gather(up_bias, "fsdp", axis=1, tiled=True),
                lax.all_gather(down_weight, "fsdp", axis=1, tiled=True),
            )
        )
        grad_mlp = cotangent[mb_index].reshape(row_count, model_width)
        grad_out = grad_mlp.astype(f32)
        down_shift_acc = down_shift_acc + jnp.sum(grad_out, axis=0)
        down_acc = down_acc + jnp.einsum(
            "rf,rd->fd", activated, grad_mlp, preferred_element_type=f32
        )
        grad_act = jnp.einsum("rd,fd->rf", grad_mlp, down_mat, preferred_element_type=f32)
        grad_pre = gelu_pull(grad_act)[0].astype(bf16)
        up_shift_acc = up_shift_acc + jnp.sum(grad_pre.astype(f32), axis=0)
        up_acc = up_acc + jnp.einsum("rd,rf->df", act_two, grad_pre, preferred_element_type=f32)
        grad_two = lax.psum(
            jnp.einsum("rf,df->rd", grad_pre, up_mat, preferred_element_type=f32).astype(
                jnp.bfloat16
            ),
            "tensor",
        ).astype(jnp.float32)
        grad_norm_in, gain_two_step, shift_two_step = norm_two_pull(grad_two)
        gain_two_acc = gain_two_acc + gain_two_step
        shift_two_acc = shift_two_acc + shift_two_step
        grad_hidden = grad_out + grad_norm_in
        qkv_mat, qv_shift, out_mat = unpack_attn(
            (
                lax.all_gather(qkv_weight, "fsdp", axis=0, tiled=True),
                lax.all_gather(qv_bias, "fsdp", axis=1, tiled=True),
                lax.all_gather(out_weight, "fsdp", axis=1, tiled=True),
            ),
            model_width,
        )
        grad_branch = grad_hidden.astype(bf16)
        out_shift_acc = out_shift_acc + jnp.sum(grad_branch.astype(f32), axis=0)
        out_acc = out_acc + jnp.einsum(
            "ra,rd->ad", attended, grad_branch, preferred_element_type=f32
        )
        grad_att = (
            jnp.einsum("rd,ad->ra", grad_branch, out_mat, preferred_element_type=f32)
            .astype(bf16)
            .reshape(images_local, seq_len, heads_local, head_dim)
        )
        again_scores = (
            jnp.einsum("bshd,bthd->bhst", queries, key_rows, preferred_element_type=f32)
            * score_scale
        )
        probs_full = jnp.exp(again_scores - logsum_exp)
        probs_low = probs_full.astype(bf16)
        val_grad = jnp.einsum(
            "bhst,bshd->bthd", probs_low, grad_att, preferred_element_type=f32
        ).astype(bf16)
        prob_grad = jnp.einsum("bshd,bthd->bhst", grad_att, val_rows, preferred_element_type=f32)
        inner_sum = jnp.sum(prob_grad * probs_full, axis=-1, keepdims=True)
        score_grad = (probs_full * (prob_grad - inner_sum)).astype(bf16)
        query_grad = (
            jnp.einsum("bhst,bthd->bshd", score_grad, key_rows, preferred_element_type=f32)
            * score_scale
        ).astype(bf16)
        key_grad = (
            jnp.einsum("bhst,bshd->bthd", score_grad, queries, preferred_element_type=f32)
            * score_scale
        ).astype(bf16)
        qv_step = jnp.concatenate(
            [
                jnp.sum(query_grad.astype(f32), axis=(0, 1)),
                jnp.sum(val_grad.astype(f32), axis=(0, 1)),
            ],
            axis=-1,
        )
        qv_acc = qv_acc + qv_step
        grad_proj = jnp.concatenate([query_grad, key_grad, val_grad], axis=-1).reshape(
            row_count, qkv_cols
        )
        qkv_acc = qkv_acc + jnp.einsum("rd,rc->dc", act_one, grad_proj, preferred_element_type=f32)
        grad_one = lax.psum(
            jnp.einsum("rc,dc->rd", grad_proj, qkv_mat, preferred_element_type=f32).astype(
                jnp.bfloat16
            ),
            "tensor",
        ).astype(jnp.float32)
        grad_input_ln, gain_one_step, shift_one_step = norm_one_pull(grad_one)
        gain_one_acc = gain_one_acc + gain_one_step
        shift_one_acc = shift_one_acc + shift_one_step
        grads_in_all.append(
            (grad_hidden + grad_input_ln).reshape(images_local, seq_len, model_width)
        )
    owned = (
        lax.psum_scatter(
            qkv_acc.reshape(model_width, heads_local, 3 * head_dim).astype(jnp.bfloat16),
            "fsdp",
            scatter_dimension=0,
            tiled=True,
        ).astype(jnp.float32),
        lax.psum_scatter(
            qv_acc.astype(jnp.bfloat16), "fsdp", scatter_dimension=1, tiled=True
        ).astype(jnp.float32),
        lax.psum_scatter(
            out_acc.astype(jnp.bfloat16), "fsdp", scatter_dimension=1, tiled=True
        ).astype(jnp.float32),
        lax.psum_scatter(
            up_acc.astype(jnp.bfloat16), "fsdp", scatter_dimension=0, tiled=True
        ).astype(jnp.float32),
        lax.psum_scatter(
            up_shift_acc.reshape(1, hidden_local).astype(jnp.bfloat16),
            "fsdp",
            scatter_dimension=1,
            tiled=True,
        ).astype(jnp.float32),
        lax.psum_scatter(
            down_acc.astype(jnp.bfloat16), "fsdp", scatter_dimension=1, tiled=True
        ).astype(jnp.float32),
        lax.psum_scatter(
            gain_one_acc.astype(jnp.bfloat16), "fsdp", scatter_dimension=0, tiled=True
        ).astype(jnp.float32),
        lax.psum_scatter(
            shift_one_acc.astype(jnp.bfloat16), "fsdp", scatter_dimension=0, tiled=True
        ).astype(jnp.float32),
        lax.psum_scatter(
            out_shift_acc.astype(jnp.bfloat16), "fsdp", scatter_dimension=0, tiled=True
        ).astype(jnp.float32),
        lax.psum_scatter(
            gain_two_acc.astype(jnp.bfloat16), "fsdp", scatter_dimension=0, tiled=True
        ).astype(jnp.float32),
        lax.psum_scatter(
            shift_two_acc.astype(jnp.bfloat16), "fsdp", scatter_dimension=0, tiled=True
        ).astype(jnp.float32),
        lax.psum_scatter(
            down_shift_acc.astype(jnp.bfloat16), "fsdp", scatter_dimension=0, tiled=True
        ).astype(jnp.float32),
    )
    piece_len = model_width // (fsdp_count * tensor_count)
    piece_start = lax.axis_index("tensor") * piece_len
    vector_grads = [
        lax.dynamic_slice_in_dim(member, piece_start, piece_len, 0) for member in owned[6:]
    ]
    activations = jnp.stack(outputs_all, axis=0)
    input_grad = jnp.stack(grads_in_all, axis=0)
    return (
        activations,
        input_grad,
        vector_grads[0],
        vector_grads[1],
        owned[0],
        owned[1],
        owned[2],
        vector_grads[2],
        vector_grads[3],
        vector_grads[4],
        owned[3],
        owned[4],
        owned[5],
        vector_grads[5],
    )


def solution(mesh):
    return jax.shard_map(
        shards,
        mesh=mesh,
        in_specs=(
            P(None, "fsdp", None, None),
            P(None, "fsdp", None, None),
            P(("fsdp", "tensor")),
            P(("fsdp", "tensor")),
            P("fsdp", "tensor", None),
            P("tensor", "fsdp"),
            P("tensor", "fsdp"),
            P(("fsdp", "tensor")),
            P(("fsdp", "tensor")),
            P(("fsdp", "tensor")),
            P("fsdp", "tensor"),
            P("tensor", "fsdp"),
            P("tensor", "fsdp"),
            P(("fsdp", "tensor")),
        ),
        out_specs=(
            P(None, "fsdp", None, None),
            P(None, "fsdp", None, None),
            P(("fsdp", "tensor")),
            P(("fsdp", "tensor")),
            P("fsdp", "tensor", None),
            P("tensor", "fsdp"),
            P("tensor", "fsdp"),
            P(("fsdp", "tensor")),
            P(("fsdp", "tensor")),
            P(("fsdp", "tensor")),
            P("fsdp", "tensor"),
            P("tensor", "fsdp"),
            P("tensor", "fsdp"),
            P(("fsdp", "tensor")),
        ),
        check_vma=False,
    )
```

profile of v0, /device:TPU:0, one launch (start us, length us, event | category | flops | bytes accessed | tf_op | source)
XLA Modules:
  0.0 895.7 jit_solution(1121077081818013780)
XLA Ops:
  13.0 43.2 %all-reduce.12 = (bf16[1024]{0:T(1024)(128)(2,1)S(1)}, bf16[1024]{0:T(1024)(128)(2,1)S(1)}, bf16[1024]{0:T(1024)(128)(2,1)S(1)}, bf16[1024]{0:T(1024)(128)(2,1)S...) all-reduce(bf16[1024]{0:T(1024)(128)(2,1)S(1)} %dynamic-update-slic, ...), channel_id=1, replica_groups=mesh['fsdp'=8,'tensor'=4] {'fsdp','tensor'}, use_global_device_ids=true, to_apply=%add.1 | all-reduce | flops 6144 | bytes 24576
  56.2 21.0 %all-gather = bf16[8,16,4]{1,2,0:T(4,128)(2,1)S(1)} all-gather(bf16[1,16,4]{1,2,0:T(4,128)(2,1)} %bitcast.357), channel_id=1, replica_groups=mesh['fsdp'=8,'tensor'=4] {'fsdp'}, dimensions={0}, use_global_device_ids=true | all-gather | bytes 1152 | tf_op jit(solution)/shard_map/all_gather | solution.py:84
  77.2 6.4 fusion.181
  85.6 27.5 %all_gather.54 = bf16[256,1024]{1,0:T(8,128)(2,1)S(1)} all-gather(bf16[256,128]{1,0:T(8,128)(2,1)S(1)} %copy-done.45), channel_id=1, replica_groups=mesh['fsdp'=8,'tensor'=4] {'fsdp'}, dimensions={1}, use_global_device_ids=true | all-gather | bytes 589824 | tf_op jit(solution)/shard_map/all_gather | solution.py:85
  131.0 16.7 %all_gather.59 = bf16[1,1024]{1,0:T(2,128)(2,1)S(1)} all-gather(bf16[1,128]{1,0:T(2,128)(2,1)S(1)} %copy-done.57), channel_id=1, replica_groups=mesh['fsdp'=8,'tensor'=4] {'fsdp'}, dimensions={1}, use_global_device_ids=true | all-gather | bytes 2304 | tf_op jit(solution)/shard_map/all_gather | solution.py:117
  147.6 6.5 fusion.180
  157.4 25.4 %all-reduce.27.cloned.1.call-done = (bf16[577,1024]{1,0:T(8,128)(2,1)}, bf16[577,1024]{1,0:T(8,128)(2,1)}) async-done(((bf16[577,1024]{1,0:T(8,128)(2,1)}, bf16[577,1024]{1,0:T(8,128)(2,1)}), (bf16[577,1024]{1,0:T(8,128)(2,1)}, bf16[577,1024]{1,0:T(8,128)(2,1)})) %all-reduce.27.cloned.1.call-update) | async-done | bytes 2363408 | tf_op jit(solution)/shard_map/psum | solution.py:113
  186.1 48.1 %all-gather.7.cloned.1.call-done = bf16[1024,1024]{1,0:T(8,128)(2,1)} async-done(((bf16[128,1024]{1,0:T(8,128)(2,1)}), bf16[1024,1024]{1,0:T(8,128)(2,1)}) %all-gather.7.cloned.1.call-update) | async-done | bytes 2097168 | tf_op jit(solution)/shard_map/all_gather | solution.py:116
  234.2 5.3 fusion.169
  239.5 45.5 %all-gather.9.cloned.1.call-done = bf16[1024,1024]{1,0:T(8,128)(2,1)} async-done(((bf16[1024,128]{1,0:T(8,128)(2,1)}), bf16[1024,1024]{1,0:T(8,128)(2,1)}) %all-gather.9.cloned.1.call-update) | async-done | bytes 2097168 | tf_op jit(solution)/shard_map/all_gather | solution.py:118
  285.0 10.2 %convert_reduce_fusion.8 = (f32[1024]{0:T(1024)S(1)}, bf16[577,1024]{1,0:T(8,128)(2,1)S(1)}, f32[577,1024]{1,0:T(8,128)}) fusion(f32[577,1024]{1,0:T(8,128)} %fusion.169, f32[1024]{0:T(1024)S(1)} %bitcast.353, bf16[577,1024]{1,0:T(8,128)(2,1)} %get-tuple-element.116, bf16[1024,1024]{1,0:T(8,128)(2,1)} %all-gather.9.cloned.1.call-done), kind=kOutput, calls=%fused_computation.107 | convolution fusion | flops 1254369280 | bytes 9195520 | tf_op jit(solution)/shard_map/rd,fd->rf/dot_general | solution.py:143
  298.9 36.0 %all-reduce.23.cloned.1.call-done = bf16[577,1024]{1,0:T(8,128)(2,1)} async-done(((bf16[577,1024]{1,0:T(8,128)(2,1)}), bf16[577,1024]{1,0:T(8,128)(2,1)}) %all-reduce.23.cloned.1.call-update) | async-done | bytes 1181712 | tf_op jit(solution)/shard_map/psum | solution.py:147
  340.7 8.0 convert_reduce_fusion.9
  353.5 6.5 multiply_convert_fusion.3
  360.0 4.6 convolution_convert_fusion.7
  367.1 23.3 %all-reduce.21.cloned.1.call-done = bf16[577,1024]{1,0:T(8,128)(2,1)} async-done(((bf16[577,1024]{1,0:T(8,128)(2,1)}), bf16[577,1024]{1,0:T(8,128)(2,1)}) %all-reduce.21.cloned.1.call-update) | async-done | bytes 1181712 | tf_op jit(solution)/shard_map/psum | solution.py:147
  390.4 4.9 convert_reduce_fusion.5
  406.0 4.6 convert_reduce_fusion.12
  410.6 7.0 multiply_reduce_fusion
  418.8 4.8 convert_reduce_fusion.14
  423.6 6.8 multiply_reduce_fusion.1
  431.0 4.3 multiply_convert_fusion
  438.3 4.1 multiply_convert_fusion.1
  482.2 4.0 fusion.167
  491.4 22.1 %reduce-scatter.21.cloned.1.call-done = bf16[16,4]{1,0:T(8,128)(2,1)} async-done(((bf16[128,4]{1,0:T(8,128)(2,1)}), bf16[16,4]{1,0:T(8,128)(2,1)}) %reduce-scatter.21.cloned.1.call-update) | async-done | bytes 144
  514.8 64.3 %reduce-scatter.23.cloned.1.call-done = bf16[128,256]{1,0:T(8,128)(2,1)} async-done(((bf16[1024,256]{1,0:T(8,128)(2,1)}), bf16[128,256]{1,0:T(8,128)(2,1)}) %reduce-scatter.23.cloned.1.call-update) | async-done | bytes 65552
  580.7 95.5 %all-reduce.25.cloned.1.call-done = (bf16[577,1024]{1,0:T(8,128)(2,1)}, bf16[577,1024]{1,0:T(8,128)(2,1)}, bf16[577,1024]{1,0:T(8,128)(2,1)}, bf16[577,1024]{1,0:T(8,128)(2,1)}) async-done(((bf16[577,1024]{1,0:T(8,128)(2,1)}, bf16[577,1024]{1,0:T(8,128)(2,1)}, bf16[577,1024]{1,0:T(8,128)(2,1)}, bf16[577,1024]{1,0:T(8,128)(2,1)}), (bf16[577,1024]{1,0:T(8,128)(2,1)}, bf16[577,1024]{1,0:T(8,128)(2,1)}, ...) | async-done | bytes 4726800 | tf_op jit(solution)/shard_map/psum | solution.py:127
  682.3 37.6 %all-reduce.13 = (bf16[1024]{0:T(1024)(128)(2,1)S(1)}, bf16[1024]{0:T(1024)(128)(2,1)S(1)}, bf16[1024]{0:T(1024)(128)(2,1)S(1)}, bf16[1024]{0:T(1024)(128)(2,1)S...) all-reduce(bf16[1024]{0:T(1024)(128)(2,1)S(1)} %add_convert_fusion., ...), channel_id=2, replica_groups=mesh['fsdp'=8,'tensor'=4] {'fsdp'}, use_global_device_ids=true, to_apply=%region_32.0.clone | all-reduce | flops 6144 | bytes 24576
  723.9 5.4 add_bitcast_fusion.1
  735.3 9.4 %copy.96 = f32[2,1,577,1024]{3,1,2,0:T(1,128)} copy(f32[2,1,577,1024]{3,2,1,0:T(8,128)} %pad_maximum_fusion) | data formatting | bytes 9453568
  752.3 63.8 %reduce-scatter.27.cloned.1.call-done = bf16[128,1024]{1,0:T(8,128)(2,1)} async-done(((bf16[1024,1024]{1,0:T(8,128)(2,1)}), bf16[128,1024]{1,0:T(8,128)(2,1)}) %reduce-scatter.27.cloned.1.call-update) | async-done | bytes 262160
  818.0 68.9 %reduce-scatter.17.cloned.1.call-done = bf16[128,1024]{1,0:T(8,128)(2,1)} async-done(((bf16[1024,1024]{1,0:T(8,128)(2,1)}), bf16[128,1024]{1,0:T(8,128)(2,1)}) %reduce-scatter.17.cloned.1.call-update) | async-done | bytes 262160 | tf_op jit(solution)/shard_map/reduce_scatter | solution.py:232
  (301 shorter events, 138.0 us)
Async XLA Ops:
  7.2 106.0 %all-gather.5.cloned.1.call-start = ((), (), s32[]{:S(2)}) async-start(), calls=%async_computation.6 | async-start | bytes 1769472 | tf_op jit(solution)/shard_map/all_gather | solution.py:83
  7.9 174.9 %all-reduce.27.cloned.1.call-start = ((), (), s32[]{:S(2)}) async-start(), calls=%async_computation.18 | async-start | bytes 4784128 | tf_op jit(solution)/shard_map/psum | solution.py:113
  56.2 61.4 %copy-start.54 = (f32[1024]{0:T(1024)}, f32[1024]{0:T(1024)S(1)}, u32[]{:S(2)}) copy-start(f32[1024]{0:T(1024)S(1)} %convert_element_type.440) | copy-start | bytes 12292
  56.2 61.4 %copy-start.39 = (f32[1024]{0:T(1024)}, f32[1024]{0:T(1024)S(1)}, u32[]{:S(2)}) copy-start(f32[1024]{0:T(1024)S(1)} %convert_element_type.439) | copy-start | bytes 12292
  84.5 31.8 %copy-start.43 = (f32[577]{0:T(1024)}, f32[577]{0:T(1024)S(1)}, u32[]{:S(2)}) copy-start(f32[577]{0:T(1024)S(1)} %broadcast_multiply_fusion.3) | copy-start | bytes 6928
  85.0 31.3 %copy-start.46 = (f32[577]{0:T(1024)}, f32[577]{0:T(1024)S(1)}, u32[]{:S(2)}) copy-start(f32[577]{0:T(1024)S(1)} %fusion.36) | copy-start | bytes 6928
  85.0 32.5 %copy-start.41 = (f32[577]{0:T(1024)}, f32[577]{0:T(1024)S(1)}, u32[]{:S(2)}) copy-start(f32[577]{0:T(1024)S(1)} %broadcast_multiply_fusion.1) | copy-start | bytes 6928
  85.5 30.8 %copy-start.48 = (f32[577]{0:T(1024)}, f32[577]{0:T(1024)S(1)}, u32[]{:S(2)}) copy-start(f32[577]{0:T(1024)S(1)} %fusion.34) | copy-start | bytes 6928
  85.6 30.7 %copy-start.52 = (f32[577]{0:T(1024)}, f32[577]{0:T(1024)S(1)}, u32[]{:S(2)}) copy-start(f32[577]{0:T(1024)S(1)} %fusion.158) | copy-start | bytes 6928
  85.6 32.0 %copy-start.50 = (f32[577]{0:T(1024)}, f32[577]{0:T(1024)S(1)}, u32[]{:S(2)}) copy-start(f32[577]{0:T(1024)S(1)} %fusion.160) | copy-start | bytes 6928
  116.3 6.1 copy-start.21
  129.6 104.6 %all-gather.7.cloned.1.call-start = ((), (), s32[]{:S(2)}) async-start(), calls=%async_computation.7 | async-start | bytes 2359296 | tf_op jit(solution)/shard_map/all_gather | solution.py:116
  130.3 154.7 %all-gather.9.cloned.1.call-start = ((), (), s32[]{:S(2)}) async-start(), calls=%async_computation.8 | async-start | bytes 2359296 | tf_op jit(solution)/shard_map/all_gather | solution.py:118
  130.9 204.0 %all-reduce.23.cloned.1.call-start = ((), (), s32[]{:S(2)}) async-start(), calls=%async_computation.10 | async-start | bytes 2392064 | tf_op jit(solution)/shard_map/psum | solution.py:147
  285.0 11.3 %copy-start.60 = (bf16[1024,1024]{1,0:T(8,128)(2,1)S(1)}, bf16[1024,1024]{1,0:T(8,128)(2,1)}, u32[]{:S(2)}) copy-start(bf16[1024,1024]{1,0:T(8,128)(2,1)} %all-gather.7.cloned.1.call-done) | copy-start | bytes 6291460
  298.8 91.6 %all-reduce.21.cloned.1.call-start = ((), (), s32[]{:S(2)}) async-start(), calls=%async_computation.9 | async-start | bytes 2392064 | tf_op jit(solution)/shard_map/psum | solution.py:147
  340.7 8.1 copy-start.27
  352.3 137.7 %reduce-scatter.25.cloned.1.call-start = ((), (), s32[]{:S(2)}) async-start(), calls=%async_computation.15 | async-start | bytes 294912
  360.0 153.5 %reduce-scatter.21.cloned.1.call-start = ((), (), s32[]{:S(2)}) async-start(), calls=%async_computation.13 | async-start | bytes 36864
  390.4 6.6 copy-start.17
  418.7 12.2 %slice-start.2 = ((s8[5980160]{0:T(1024)(128)(4,1)}), s8[4194304]{0:T(1024)(128)(4,1)S(1)}, s32[]{:S(2)}) async-start(s8[5980160]{0:T(1024)(128)(4,1)} %bitcast.331), calls=%async_computation.21 | async-start | bytes 8388608
  423.5 6.8 copy-start.25
  423.5 6.8 copy-start.26
  423.5 7.5 slice-start.3
  431.0 7.4 slice-start
  431.0 7.3 slice-start.1
  435.3 7.1 copy-start.9
  446.3 132.7 %reduce-scatter.23.cloned.1.call-start = ((), (), s32[]{:S(2)}) async-start(), calls=%async_computation.14 | async-start | bytes 589824
  451.2 225.0 %all-reduce.25.cloned.1.call-start = ((), (), s32[]{:S(2)}) async-start(), calls=%async_computation.17 | async-start | bytes 9568256 | tf_op jit(solution)/shard_map/psum | solution.py:127
  460.6 289.8 %reduce-scatter.19.cloned.1.call-start = ((), (), s32[]{:S(2)}) async-start(), calls=%async_computation.12 | async-start | bytes 1769472
  469.5 346.6 %reduce-scatter.27.cloned.1.call-start = ((), (), s32[]{:S(2)}) async-start(), calls=%async_computation.16 | async-start | bytes 2359296
  480.6 406.4 %reduce-scatter.17.cloned.1.call-start = ((), (), s32[]{:S(2)}) async-start(), calls=%async_computation.11 | async-start | bytes 2359296 | tf_op jit(solution)/shard_map/reduce_scatter | solution.py:232
  (53 other events, 175.0 us)
Sparse Core Ops, SparseCore 0:
  10.0 47.7 all-gather.4
  129.7 53.1 all-reduce.26
  185.0 49.1 all-gather.6
  236.1 48.8 all-gather.8
  298.9 35.9 all-reduce.22
  352.4 37.8 all-reduce.20
  393.7 62.2 reduce-scatter.24
  459.7 53.7 reduce-scatter.20
  517.4 61.6 reduce-scatter.22
  582.1 94.1 all-reduce.24
  679.6 65.7 reduce-scatter.18
  748.8 67.2 reduce-scatter.26
  819.6 67.3 reduce-scatter.16
where the time goes:
time: 903 us; the launch traced here: 896 us
  waiting for transfers between devices  495 us (55%)
  blocking collectives  146 us (16%)
  matrix products  115 us (13%)
  other arithmetic  65.3 us (7%)
  local copies, waits for them, and re-layouts  57.5 us (6%)
  between operations  16.2 us (2%)
    unnamed x18, waiting for transfers between devices  152 us
    psum x1, waiting for transfers between devices, shards(): lax.psum(mlp_part.astype(jnp.bfloat16), 'tensor').astype(jnp.float32)  95.5 us
    unnamed x2, blocking collectives  80.7 us
    reduce_scatter x1, waiting for transfers between devices, shards(): lax.psum_scatter(up_acc.astype(jnp.bfloat16), 'fsdp', scatter_dimension=0...  68.9 us
    psum x2, waiting for transfers between devices, shards(): lax.psum(jnp.einsum('rf,df->rd', grad_pre, up_mat, preferred_element_type...  59.3 us
    all_gather x1, waiting for transfers between devices, shards(): lax.all_gather(up_weight, 'fsdp', axis=0, tiled=True)  48.1 us
    all_gather x1, waiting for transfers between devices, shards(): lax.all_gather(down_weight, 'fsdp', axis=1, tiled=True)  45.5 us
    unnamed x169, local copies, waits for them, and re-layouts  38.6 us
  transfers between devices with their start and end apart: 13, of which 10 were waited for; matrix products, arithmetic and copies ran while one was open for 21% of the time, Pallas kernels for 0%

commit v1 on v0

--- a/solution.py
+++ b/solution.py
@@ -1,9 +1,17 @@
+import functools
 import jax
 import jax.numpy as jnp
 from jax import lax
 from jax.sharding import PartitionSpec as P
 
 epsilon = 1e-06
+
+
+def packet_feed(chunk, mesh_dim):
+    return jnp.sum(lax.all_gather(chunk, mesh_dim), 0)
+
+
+state_sample_for = functools.partial(packet_feed, mesh_dim="tensor")
 
 
 def layer_norm(values, scale_vec, shift_vec):
@@ -124,7 +132,7 @@
         gelu_full, gelu_pull = jax.vjp(gelu_exact, pre_act)
         activated = gelu_full.astype(bf16)
         mlp_part = jnp.dot(activated, down_mat, preferred_element_type=f32)
-        mlp_total = lax.psum(mlp_part.astype(jnp.bfloat16), "tensor").astype(jnp.float32)
+        mlp_total = state_sample_for(mlp_part.astype(jnp.bfloat16)).astype(jnp.float32)
         output_rows = (hidden_res + (mlp_total + down_shift)).astype(bf16)
         outputs_all.append(output_rows.reshape(images_local, seq_len, model_width))
         up_mat, up_shift, down_mat = unpack_mlp(

time: 903 us -> 972 us (1.076)
  waiting for transfers between devices: 495 us -> 551 us
  other arithmetic: 65.3 us -> 75.6 us
    all_gather x0 -> x2, waiting for transfers between devices: none -> 71 us  [packet_feed(): return jnp.sum(lax.all_gather(chunk, mesh_dim), 0)]
    psum x1, waiting for transfers between devices: 95.5 us -> 55.8 us  [shards(): lax.psum(jnp.einsum('rc,dc->rd', grad_proj, qkv_mat, preferred_element_ty...]
    unnamed x18 -> x20, waiting for transfers between devices: 152 us -> 167 us
    psum x2, waiting for transfers between devices: 59.3 us -> 69.3 us  [shards(): lax.psum(jnp.einsum('rf,df->rd', grad_pre, up_mat, preferred_element_type...]
    unnamed x169 -> x171, local copies, waits for them, and re-layouts: 38.6 us -> 38.8 us
  transfers between devices with their start and end apart: 13 -> 15, of which waited for: 10 -> 13; matrix products, arithmetic and copies ran while one was open for 21% -> 17% of each run, Pallas kernels for 0% -> 0%
where the time goes in v1:
time: 972 us; the launch traced here: 965 us
  waiting for transfers between devices  551 us (57%)
  blocking collectives  146 us (15%)
  matrix products  115 us (12%)
  other arithmetic  75.6 us (8%)
  local copies, waits for them, and re-layouts  59.2 us (6%)
  between operations  16 us (2%)
    unnamed x20, waiting for transfers between devices  167 us
    unnamed x2, blocking collectives  80.9 us
    all_gather x2, waiting for transfers between devices, packet_feed(): return jnp.sum(lax.all_gather(chunk, mesh_dim), 0)  71 us
    reduce_scatter x1, waiting for transfers between devices, shards(): lax.psum_scatter(up_acc.astype(jnp.bfloat16), 'fsdp', scatter_dimension=0...  69.7 us
    psum x2, waiting for transfers between devices, shards(): lax.psum(jnp.einsum('rf,df->rd', grad_pre, up_mat, preferred_element_type...  69.3 us
    psum x1, waiting for transfers between devices, shards(): lax.psum(jnp.einsum('rc,dc->rd', grad_proj, qkv_mat, preferred_element_ty...  55.8 us
    all_gather x1, waiting for transfers between devices, shards(): lax.all_gather(up_weight, 'fsdp', axis=0, tiled=True)  48.1 us
    all_gather x1, waiting for transfers between devices, shards(): lax.all_gather(down_weight, 'fsdp', axis=1, tiled=True)  45.4 us
  transfers between devices with their start and end apart: 15, of which 13 were waited for; matrix products, arithmetic and copies ran while one was open for 17% of the time, Pallas kernels for 0%

profile of v1, /device:TPU:0, one launch (start us, length us, event | category | flops | bytes accessed | tf_op | source)
XLA Modules:
  0.0 964.7 jit_solution(11525278804507011988)
XLA Ops:
  13.0 43.2 %all-reduce.12 = (bf16[1024]{0:T(1024)(128)(2,1)S(1)}, bf16[1024]{0:T(1024)(128)(2,1)S(1)}, bf16[1024]{0:T(1024)(128)(2,1)S(1)}, bf16[1024]{0:T(1024)(128)(2,1)S...) all-reduce(bf16[1024]{0:T(1024)(128)(2,1)S(1)} %dynamic-update-slic, ...), channel_id=1, replica_groups=mesh['fsdp'=8,'tensor'=4] {'fsdp','tensor'}, use_global_device_ids=true, to_apply=%add.1 | all-reduce | flops 6144 | bytes 24576
  56.2 21.0 %all-gather.2 = bf16[8,16,4]{1,2,0:T(4,128)(2,1)S(1)} all-gather(bf16[1,16,4]{1,2,0:T(4,128)(2,1)} %bitcast.361), channel_id=1, replica_groups=mesh['fsdp'=8,'tensor'=4] {'fsdp'}, dimensions={0}, use_global_device_ids=true | all-gather | bytes 1152 | tf_op jit(solution)/shard_map/all_gather | solution.py:92
  77.2 6.5 fusion.183
  85.7 27.6 %all_gather.66 = bf16[256,1024]{1,0:T(8,128)(2,1)S(1)} all-gather(bf16[256,128]{1,0:T(8,128)(2,1)S(1)} %copy-done.46), channel_id=1, replica_groups=mesh['fsdp'=8,'tensor'=4] {'fsdp'}, dimensions={1}, use_global_device_ids=true | all-gather | bytes 589824 | tf_op jit(solution)/shard_map/all_gather | solution.py:93
  131.1 16.8 %all_gather.71 = bf16[1,1024]{1,0:T(2,128)(2,1)S(1)} all-gather(bf16[1,128]{1,0:T(2,128)(2,1)S(1)} %copy-done.59), channel_id=1, replica_groups=mesh['fsdp'=8,'tensor'=4] {'fsdp'}, dimensions={1}, use_global_device_ids=true | all-gather | bytes 2304 | tf_op jit(solution)/shard_map/all_gather | solution.py:125
  147.9 7.9 fusion.182
  158.0 24.9 %all-reduce.27.cloned.1.call-done = (bf16[577,1024]{1,0:T(8,128)(2,1)}, bf16[577,1024]{1,0:T(8,128)(2,1)}) async-done(((bf16[577,1024]{1,0:T(8,128)(2,1)}, bf16[577,1024]{1,0:T(8,128)(2,1)}), (bf16[577,1024]{1,0:T(8,128)(2,1)}, bf16[577,1024]{1,0:T(8,128)(2,1)})) %all-reduce.27.cloned.1.call-update) | async-done | bytes 2363408 | tf_op jit(solution)/shard_map/psum | solution.py:121
  186.2 48.1 %all-gather.13.cloned.1.call-done = bf16[1024,1024]{1,0:T(8,128)(2,1)} async-done(((bf16[128,1024]{1,0:T(8,128)(2,1)}), bf16[1024,1024]{1,0:T(8,128)(2,1)}) %all-gather.13.cloned.1.call-update) | async-done | bytes 2097168 | tf_op jit(solution)/shard_map/all_gather | solution.py:124
  234.3 5.4 fusion.171
  239.7 45.4 %all-gather.15.cloned.1.call-done = bf16[1024,1024]{1,0:T(8,128)(2,1)} async-done(((bf16[1024,128]{1,0:T(8,128)(2,1)}), bf16[1024,1024]{1,0:T(8,128)(2,1)}) %all-gather.15.cloned.1.call-update) | async-done | bytes 2097168 | tf_op jit(solution)/shard_map/all_gather | solution.py:126
  285.1 10.2 %convert_reduce_fusion.8 = (f32[1024]{0:T(1024)S(1)}, bf16[577,1024]{1,0:T(8,128)(2,1)S(1)}, f32[577,1024]{1,0:T(8,128)}) fusion(f32[577,1024]{1,0:T(8,128)} %fusion.171, f32[1024]{0:T(1024)S(1)} %bitcast.357, bf16[577,1024]{1,0:T(8,128)(2,1)} %get-tuple-element.114, bf16[1024,1024]{1,0:T(8,128)(2,1)} %all-gather.15.cloned.1.call-done), kind=kOutput, calls=%fused_computation.107 | convolution fusion | flops 1254369280 | bytes 9195520 | tf_op jit(solution)/shard_map/rd,fd->rf/dot_general | solution.py:151
  302.2 32.7 %all-reduce.23.cloned.1.call-done = bf16[577,1024]{1,0:T(8,128)(2,1)} async-done(((bf16[577,1024]{1,0:T(8,128)(2,1)}), bf16[577,1024]{1,0:T(8,128)(2,1)}) %all-reduce.23.cloned.1.call-update) | async-done | bytes 1181712 | tf_op jit(solution)/shard_map/psum | solution.py:155
  340.8 8.0 convert_reduce_fusion.9
  353.9 36.5 %all-reduce.21.cloned.1.call-done = bf16[577,1024]{1,0:T(8,128)(2,1)} async-done(((bf16[577,1024]{1,0:T(8,128)(2,1)}), bf16[577,1024]{1,0:T(8,128)(2,1)}) %all-reduce.21.cloned.1.call-update) | async-done | bytes 1181712 | tf_op jit(solution)/shard_map/psum | solution.py:155
  390.4 4.9 convert_reduce_fusion.5
  410.2 6.9 multiply_reduce_fusion
  418.3 4.8 convert_reduce_fusion.14
  423.1 6.9 multiply_reduce_fusion.1
  469.3 5.2 multiply_convert_fusion.3
  503.7 9.9 %reduce-scatter.21.cloned.1.call-done = bf16[16,4]{1,0:T(8,128)(2,1)} async-done(((bf16[128,4]{1,0:T(8,128)(2,1)}), bf16[16,4]{1,0:T(8,128)(2,1)}) %reduce-scatter.21.cloned.1.call-update) | async-done | bytes 144
  514.9 64.3 %reduce-scatter.23.cloned.1.call-done = bf16[128,256]{1,0:T(8,128)(2,1)} async-done(((bf16[1024,256]{1,0:T(8,128)(2,1)}), bf16[128,256]{1,0:T(8,128)(2,1)}) %reduce-scatter.23.cloned.1.call-update) | async-done | bytes 65552
  580.8 55.8 %all-reduce.25.cloned.1.call-done = (bf16[577,1024]{1,0:T(8,128)(2,1)}, bf16[577,1024]{1,0:T(8,128)(2,1)}) async-done(((bf16[577,1024]{1,0:T(8,128)(2,1)}, bf16[577,1024]{1,0:T(8,128)(2,1)}), (bf16[577,1024]{1,0:T(8,128)(2,1)}, bf16[577,1024]{1,0:T(8,128)(2,1)})) %all-reduce.25.cloned.1.call-update) | async-done | bytes 2363408 | tf_op jit(solution)/shard_map/psum | solution.py:215
  642.8 37.8 %all-reduce.13 = (bf16[1024]{0:T(1024)(128)(2,1)S(1)}, bf16[1024]{0:T(1024)(128)(2,1)S(1)}, bf16[1024]{0:T(1024)(128)(2,1)S(1)}, bf16[1024]{0:T(1024)(128)(2,1)S...) all-reduce(bf16[1024]{0:T(1024)(128)(2,1)S(1)} %add_convert_fusion., ...), channel_id=4, replica_groups=mesh['fsdp'=8,'tensor'=4] {'fsdp'}, use_global_device_ids=true, to_apply=%region_32.0.clone | all-reduce | flops 6144 | bytes 24576
  684.5 21.5 %reduce-scatter.19.cloned.1.call-done = bf16[128,768]{1,0:T(8,128)(2,1)} async-done(((bf16[1024,768]{1,0:T(8,128)(2,1)}), bf16[128,768]{1,0:T(8,128)(2,1)}) %reduce-scatter.19.cloned.1.call-update) | async-done | bytes 196624
  707.9 69.3 %reduce-scatter.27.cloned.1.call-done = bf16[128,1024]{1,0:T(8,128)(2,1)} async-done(((bf16[1024,1024]{1,0:T(8,128)(2,1)}), bf16[128,1024]{1,0:T(8,128)(2,1)}) %reduce-scatter.27.cloned.1.call-update) | async-done | bytes 262160
  779.2 69.7 %reduce-scatter.17.cloned.1.call-done = bf16[128,1024]{1,0:T(8,128)(2,1)} async-done(((bf16[1024,1024]{1,0:T(8,128)(2,1)}), bf16[128,1024]{1,0:T(8,128)(2,1)}) %reduce-scatter.17.cloned.1.call-update) | async-done | bytes 262160 | tf_op jit(solution)/shard_map/reduce_scatter | solution.py:240
  850.6 36.6 %all-gather.19.cloned.1.call-done = bf16[4,577,1024]{2,1,0:T(8,128)(2,1)} async-done(((bf16[1,577,1024]{2,1,0:T(8,128)(2,1)}), bf16[4,577,1024]{2,1,0:T(8,128)(2,1)}) %all-gather.19.cloned.1.call-update) | async-done | bytes 4726800 | tf_op jit(solution)/shard_map/all_gather | solution.py:11
  887.2 4.8 reduce_sum.379
  892.0 34.4 %all-gather.17.cloned.1.call-done = bf16[4,577,1024]{2,1,0:T(8,128)(2,1)} async-done(((bf16[1,577,1024]{2,1,0:T(8,128)(2,1)}), bf16[4,577,1024]{2,1,0:T(8,128)(2,1)}) %all-gather.17.cloned.1.call-update) | async-done | bytes 4726800 | tf_op jit(solution)/shard_map/all_gather | solution.py:11
  926.5 4.8 reduce_sum.370
  931.3 5.4 add_bitcast_fusion.1
  942.9 9.4 copy.96
  (311 shorter events, 162.1 us)
Async XLA Ops:
  7.2 106.1 %all-gather.11.cloned.1.call-start = ((), (), s32[]{:S(2)}) async-start(), calls=%async_computation.6 | async-start | bytes 1769472 | tf_op jit(solution)/shard_map/all_gather | solution.py:91
  7.9 175.0 %all-reduce.27.cloned.1.call-start = ((), (), s32[]{:S(2)}) async-start(), calls=%async_computation.20 | async-start | bytes 4784128 | tf_op jit(solution)/shard_map/psum | solution.py:121
  56.2 61.5 %copy-start.56 = (f32[1024]{0:T(1024)}, f32[1024]{0:T(1024)S(1)}, u32[]{:S(2)}) copy-start(f32[1024]{0:T(1024)S(1)} %convert_element_type.444) | copy-start | bytes 12292
  56.2 61.5 %copy-start.40 = (f32[1024]{0:T(1024)}, f32[1024]{0:T(1024)S(1)}, u32[]{:S(2)}) copy-start(f32[1024]{0:T(1024)S(1)} %convert_element_type.443) | copy-start | bytes 12292
  84.6 31.8 %copy-start.44 = (f32[577]{0:T(1024)}, f32[577]{0:T(1024)S(1)}, u32[]{:S(2)}) copy-start(f32[577]{0:T(1024)S(1)} %broadcast_multiply_fusion.3) | copy-start | bytes 6928
  85.1 31.4 %copy-start.47 = (f32[577]{0:T(1024)}, f32[577]{0:T(1024)S(1)}, u32[]{:S(2)}) copy-start(f32[577]{0:T(1024)S(1)} %fusion.36) | copy-start | bytes 6928
  85.1 32.6 %copy-start.42 = (f32[577]{0:T(1024)}, f32[577]{0:T(1024)S(1)}, u32[]{:S(2)}) copy-start(f32[577]{0:T(1024)S(1)} %broadcast_multiply_fusion.1) | copy-start | bytes 6928
  85.5 30.9 %copy-start.49 = (f32[577]{0:T(1024)}, f32[577]{0:T(1024)S(1)}, u32[]{:S(2)}) copy-start(f32[577]{0:T(1024)S(1)} %fusion.34) | copy-start | bytes 6928
  85.6 30.8 %copy-start.53 = (f32[577]{0:T(1024)}, f32[577]{0:T(1024)S(1)}, u32[]{:S(2)}) copy-start(f32[577]{0:T(1024)S(1)} %fusion.160) | copy-start | bytes 6928
  85.7 32.0 %copy-start.51 = (f32[577]{0:T(1024)}, f32[577]{0:T(1024)S(1)}, u32[]{:S(2)}) copy-start(f32[577]{0:T(1024)S(1)} %fusion.162) | copy-start | bytes 6928
  129.7 104.6 %all-gather.13.cloned.1.call-start = ((), (), s32[]{:S(2)}) async-start(), calls=%async_computation.7 | async-start | bytes 2359296 | tf_op jit(solution)/shard_map/all_gather | solution.py:124
  130.4 154.7 %all-gather.15.cloned.1.call-start = ((), (), s32[]{:S(2)}) async-start(), calls=%async_computation.8 | async-start | bytes 2359296 | tf_op jit(solution)/shard_map/all_gather | solution.py:126
  131.0 204.0 %all-reduce.23.cloned.1.call-start = ((), (), s32[]{:S(2)}) async-start(), calls=%async_computation.10 | async-start | bytes 2392064 | tf_op jit(solution)/shard_map/psum | solution.py:155
  285.1 11.3 %copy-start.61 = (bf16[1024,1024]{1,0:T(8,128)(2,1)S(1)}, bf16[1024,1024]{1,0:T(8,128)(2,1)}, u32[]{:S(2)}) copy-start(bf16[1024,1024]{1,0:T(8,128)(2,1)} %all-gather.13.cloned.1.call-done) | copy-start | bytes 6291460
  298.8 91.6 %all-reduce.21.cloned.1.call-start = ((), (), s32[]{:S(2)}) async-start(), calls=%async_computation.9 | async-start | bytes 2392064 | tf_op jit(solution)/shard_map/psum | solution.py:155
  340.8 8.0 copy-start.29
  352.4 149.9 %reduce-scatter.25.cloned.1.call-start = ((), (), s32[]{:S(2)}) async-start(), calls=%async_computation.17 | async-start | bytes 294912
  353.4 160.2 %reduce-scatter.21.cloned.1.call-start = ((), (), s32[]{:S(2)}) async-start(), calls=%async_computation.15 | async-start | bytes 36864
  418.3 12.3 %slice-start.2 = ((s8[5980160]{0:T(1024)(128)(4,1)}), s8[4194304]{0:T(1024)(128)(4,1)S(1)}, s32[]{:S(2)}) async-start(s8[5980160]{0:T(1024)(128)(4,1)} %bitcast.335), calls=%async_computation.23 | async-start | bytes 8388608
  423.1 6.9 copy-start.26
  423.1 6.9 copy-start.28
  423.1 7.5 slice-start.3
  430.6 7.4 slice-start
  430.6 7.3 slice-start.1
  434.9 7.1 copy-start.9
  446.0 133.3 %reduce-scatter.23.cloned.1.call-start = ((), (), s32[]{:S(2)}) async-start(), calls=%async_computation.16 | async-start | bytes 589824
  450.8 185.8 %all-reduce.25.cloned.1.call-start = ((), (), s32[]{:S(2)}) async-start(), calls=%async_computation.19 | async-start | bytes 4784128 | tf_op jit(solution)/shard_map/psum | solution.py:215
  460.3 245.8 %reduce-scatter.19.cloned.1.call-start = ((), (), s32[]{:S(2)}) async-start(), calls=%async_computation.14 | async-start | bytes 1769472
  469.2 308.0 %reduce-scatter.27.cloned.1.call-start = ((), (), s32[]{:S(2)}) async-start(), calls=%async_computation.18 | async-start | bytes 2359296
  483.9 365.0 %reduce-scatter.17.cloned.1.call-start = ((), (), s32[]{:S(2)}) async-start(), calls=%async_computation.11 | async-start | bytes 2359296 | tf_op jit(solution)/shard_map/reduce_scatter | solution.py:240
  491.9 395.3 %all-gather.19.cloned.1.call-start = ((), (), s32[]{:S(2)}) async-start(), calls=%async_computation.13 | async-start | bytes 5980160 | tf_op jit(solution)/shard_map/all_gather | solution.py:11
  496.4 430.0 %all-gather.17.cloned.1.call-start = ((), (), s32[]{:S(2)}) async-start(), calls=%async_computation.12 | async-start | bytes 5980160 | tf_op jit(solution)/shard_map/all_gather | solution.py:11
  (56 other events, 188.3 us)
Sparse Core Ops, SparseCore 0:
  10.0 47.7 all-gather.10
  129.8 53.1 all-reduce.26
  185.1 49.1 all-gather.12
  236.2 48.8 all-gather.14
  299.0 35.9 all-reduce.22
  352.5 37.8 all-reduce.20
  393.7 62.2 reduce-scatter.24
  459.7 53.8 reduce-scatter.20
  517.5 61.6 reduce-scatter.22
  581.4 55.1 all-reduce.24
  640.1 65.9 reduce-scatter.18
  710.0 67.1 reduce-scatter.26
  781.3 67.4 reduce-scatter.16
  850.3 36.8 all-gather.18
  888.6 37.7 all-gather.16
